TPU v7x, 256 devices: a whole 4x4x8 slice. The times are simulated.
256 devices in a mesh: drive: 4 (over y), brick: 64 (over x, z, core).
Axes of the slice: x: 4, y: 4, z: 8, core: 2. Of those that a mesh axis runs over, the one named last changes fastest.
Arguments:
- cam_tiles: bfloat16 [4, 1, 256, 64, 256], P('drive', None, 'brick')
- vox_embed: bfloat16 [1536, 128, 256], P('brick'), may hold values from -6 to 6
- prev_state: bfloat16 [4, 1536, 128, 256], P('drive', 'brick'), may hold values from -6 to 6
- tile_sends: int32 [4, 1, 64, 128], P('drive', None, 'brick'), may hold values from 0 to 3, as said below
- brick_tiles: int32 [4, 1, 1536, 8], P('drive', None, 'brick'), may hold values from -1 to 127, as said below
- ego_shift: int32 [4, 1], P('drive'), may hold values from 0 to 24
- norm_gains: float32 [2, 256], replicated, may hold values from 0.1 to 1.9
- w_query: bfloat16 [256, 256], replicated, may hold values from -0.375 to 0.375
- w_keyval: bfloat16 [256, 512], replicated, may hold values from -0.375 to 0.375
- w_attn_out: bfloat16 [256, 256], replicated, may hold values from -0.375 to 0.375
- w_in: bfloat16 [256, 512], replicated, may hold values from -0.375 to 0.375
- w_out: bfloat16 [512, 256], replicated, may hold values from -0.25 to 0.25
- grad_out: bfloat16 [4, 1536, 128, 256], P('drive', 'brick'), may hold values from -0.015625 to 0.015625
Outputs:
- new_state: bfloat16 [4, 1536, 128, 256], P('drive', 'brick')
- grad_w_in: float32 [256, 512], replicated
- grad_w_out: float32 [512, 256], replicated
Inputs may be any that keep to these rules, and one draw needn't show every extreme that they name: `tile_sends`: entry [drive, frame, p, d * 2 + c] is a tile of shard p, a local index, that shard p sends to shard d as its c-th slot; the 2 entries of one pair are distinct. `brick_tiles`: -1 is padding; other entries are distinct within a brick and name received slots; every brick has one or more, and in each drive and frame some brick has all 8.
All inputs are finite; a program needn't handle non-finite values.
Results may differ from a plain program's by a relative error of at most 0.0022.
The roundings to bfloat16 on the way count: a program that leaves them out, or rounds other values in their place, can miss the bound.
Values may be sent and summed in bfloat16 or wider, within the bound.
No kernel may reach another device: no remote copies, remote signals or barrier semaphores. Data moves between devices by JAX's collectives and lax.ppermute only.
A program may use at most 128 MiB of HBM per device.

v0:
```python
import jax
import jax.numpy as jnp
from jax import lax
from jax.sharding import PartitionSpec as P

HD = 32


def passed_along(value, axis, by):
    count = lax.axis_size(axis)
    pairs = [(i, i + by) for i in range(count) if 0 <= i + by < count]
    return lax.ppermute(value, axis, pairs)


def rms_norm(values, norm_gain):
    mean_sq = jnp.mean(values * values, axis=-1, keepdims=True)
    return values * lax.rsqrt(mean_sq + 1e-06) * norm_gain


def gelu_tanh(values):
    return jax.nn.gelu(values, approximate=True)


def take_rows(source_rows, positions):
    return source_rows[positions]


def on_device(
    cam_tiles,
    vox_embed,
    prev_state,
    tile_sends,
    brick_tiles,
    ego_shift,
    norm_gains,
    w_query,
    w_keyval,
    w_attn_out,
    w_in,
    w_out,
    grad_out,
):
    shards = lax.axis_size("brick")
    own_index = lax.axis_index("brick")
    frames = cam_tiles.shape[1]
    tile_dev = cam_tiles.shape[2]
    pixels = cam_tiles.shape[3]
    width = cam_tiles.shape[4]
    slots = tile_sends.shape[3]
    capacity = slots // shards
    brick_dev = vox_embed.shape[0]
    brick_size = vox_embed.shape[1]
    list_len = brick_tiles.shape[3]
    head_count = width // HD
    scale = 1.0 / HD**0.5
    group_size = min(brick_dev, max(1, 512 // brick_size))
    blocks = brick_dev // group_size
    tile_feats = cam_tiles[0]
    payload = (
        jnp.dot(tile_feats.reshape(-1, width), w_keyval, preferred_element_type=jnp.float32)
        .astype(jnp.bfloat16)
        .reshape(frames, tile_dev, pixels, 2 * width)
    )
    everything, all_plans = (
        lax.all_gather(payload, "brick", axis=1, tiled=True),
        lax.all_gather(tile_sends[0], "brick", axis=1, tiled=True),
    )
    own_plan = lax.dynamic_slice_in_dim(all_plans, own_index * capacity, capacity, 2)
    slot_index = (jnp.arange(shards, dtype=jnp.int32)[:, None] * tile_dev + own_plan).reshape(
        frames, slots
    )
    slot_data = jax.vmap(take_rows)(everything, slot_index)
    voxel_state = prev_state[0]
    behind = passed_along(voxel_state, "brick", 1)
    joined = jnp.concatenate([behind, voxel_state], 0)
    start = brick_dev - ego_shift[0, 0]
    shifted = lax.dynamic_slice_in_dim(joined, start, brick_dev, 0)
    q_in = vox_embed.astype(jnp.float32) + shifted.astype(jnp.float32)
    normed = rms_norm(q_in, norm_gains[0]).astype(jnp.bfloat16)
    queries = jnp.dot(
        normed.reshape(-1, width), w_query, preferred_element_type=jnp.float32
    ).astype(jnp.bfloat16)
    query_blocks = queries.reshape(blocks, group_size, brick_size, head_count, HD)
    keyval = slot_data[0]
    entries = brick_tiles[0, 0]

    def attend(operands):
        query_block, entry_block = operands
        gathered = keyval[jnp.maximum(entry_block, 0)].reshape(
            group_size, list_len * pixels, 2, head_count, HD
        )
        keys_part = gathered[:, :, 0]
        values_part = gathered[:, :, 1]
        scores = (
            jnp.einsum(
                "gqhd,gkhd->ghqk", query_block, keys_part, preferred_element_type=jnp.float32
            )
            * scale
        )
        live_keys = jnp.broadcast_to(
            (entry_block >= 0)[:, :, None], (group_size, list_len, pixels)
        ).reshape(group_size, 1, 1, list_len * pixels)
        scores = jnp.where(live_keys, scores, -1e30)
        row_peak = jnp.max(scores, axis=-1, keepdims=True)
        raised = jnp.exp(scores - row_peak)
        weights = (raised / jnp.sum(raised, axis=-1, keepdims=True)).astype(jnp.bfloat16)
        mixed = jnp.einsum(
            "ghqk,gkhd->gqhd", weights, values_part, preferred_element_type=jnp.float32
        )
        return mixed.astype(jnp.bfloat16)

    attended = lax.map(
        attend, (query_blocks, entries.reshape(blocks, group_size, list_len))
    ).reshape(-1, width)
    residual_x = q_in.reshape(-1, width) + jnp.dot(
        attended, w_attn_out, preferred_element_type=jnp.float32
    )
    hidden_in = rms_norm(residual_x, norm_gains[1]).astype(jnp.bfloat16)
    pre_act = jnp.dot(hidden_in, w_in, preferred_element_type=jnp.float32)
    activated = gelu_tanh(pre_act).astype(jnp.bfloat16)
    voxel_state = (
        (residual_x + jnp.dot(activated, w_out, preferred_element_type=jnp.float32))
        .astype(jnp.bfloat16)
        .reshape(brick_dev, brick_size, width)
    )
    cotangent = grad_out[0].reshape(-1, width)
    part_w_out = jnp.dot(activated.T, cotangent, preferred_element_type=jnp.float32)
    d_act = jnp.dot(cotangent, w_out.T, preferred_element_type=jnp.float32)
    unused_value, pullback = jax.vjp(gelu_tanh, pre_act)
    d_pre = pullback(d_act)[0].astype(jnp.bfloat16)
    part_w_in = jnp.dot(hidden_in.T, d_pre, preferred_element_type=jnp.float32)
    grad_w_in, grad_w_out = lax.psum((part_w_in, part_w_out), ("drive", "brick"))
    return (voxel_state[None], grad_w_in, grad_w_out)


def solution(mesh):
    return jax.shard_map(
        on_device,
        mesh=mesh,
        in_specs=(
            P("drive", None, "brick", None, None),
            P("brick", None, None),
            P("drive", "brick", None, None),
            P("drive", None, "brick", None),
            P("drive", None, "brick", None),
            P("drive", None),
            P(),
            P(),
            P(),
            P(),
            P(),
            P(),
            P("drive", "brick", None, None),
        ),
        out_specs=(P("drive", "brick", None, None), P(), P()),
        check_vma=False,
    )
```

profile of v0, /device:TPU:2, one launch (start us, length us, event | category | flops | bytes accessed | tf_op | source)
XLA Modules:
  0.0 652.4 jit_solution(17826369599442796199)
XLA Ops:
  11.9 58.8 %all-gather = s32[1,64,1,128]{3,2,0,1:T(1,128)S(1)} all-gather(s32[1,1,1,128]{3,2,0,1:T(1,128)} %bitcast.78), channel_id=2, replica_groups=mesh['drive'=4,'brick'=64] {'brick'}, dimensions={1}, use_global_device_ids=true | all-gather | bytes 33280 | tf_op jit(solution)/shard_map/all_gather | solution.py:66
  72.8 2.9 multiply_reduce_fusion.1
  80.4 4.2 reshape.122
  84.6 28.0 %all-gather.3.cloned.1.call-done = bf16[1,256,64,512]{3,2,0,1:T(8,128)(2,1)} async-done(((bf16[1,4,64,512]{3,2,0,1:T(8,128)(2,1)}), bf16[1,256,64,512]{3,2,0,1:T(8,128)(2,1)}) %all-gather.3.cloned.1.call-update) | async-done | bytes 16777232 | tf_op jit(solution)/shard_map/all_gather | solution.py:65
  112.7 12.5 %gather_fusion.1 = bf16[128,64,512]{2,1,0:T(8,128)(2,1)} fusion(bf16[1,256,64,512]{3,2,0,1:T(8,128)(2,1)} %all-gather.3.cloned.1.call-done, s32[128]{0:T(128)S(1)} %or_bitcast_fusion), kind=kCustom, calls=%fused_computation.1 | custom fusion | bytes 16778240 | tf_op jit(solution)/shard_map/vmap()/gather | solution.py:25
  125.2 235.8 %while.10 = (s32[]{:T(128)}, bf16[6,4,128,8,32]{2,1,0,4,3:T(4,128)(2,1)}, s32[6,4,8]{2,1,0:T(4,128)S(1)}, bf16[128,64,512]{2,1,0:T(8,128)(2,1)}, bf16[6,4,128,8,32]{2,1,0,4,3:T(4,128)(2,1)}, /*index=5*/s32[]{:T(128)}) while((s32[]{:T(128)}, bf16[6,4,128,8,32]{2,1,0,4,3:T(4,128)(2,1)}, s32[6,4,8]{2,1,0:T(4,128)S(1)}, ...), condition=%wide.region_4.5_spmd, body=%wide.region_1.4_spmd.sunk | while | flops 285345344 | bytes 54048272 | solution.py:112
  125.3 5.4 gather_fusion
  130.6 7.4 %copy.61 = bf16[32,64,512]{1,0,2:T(8,128)(2,1)} copy(bf16[32,64,512]{2,1,0:T(8,128)(2,1)} %gather_fusion) | data formatting | bytes 4194304 | tf_op jit(solution)/shard_map/while/body/eval_jaxpr/gather | solution.py:89
  138.1 6.7 %reshape.153 = bf16[4,512,2,8,32]{1,0,4,3,2:T(4,128)(2,1)} reshape(bf16[32,64,512]{1,0,2:T(8,128)(2,1)} %copy.61) | data formatting | bytes 4194304 | tf_op jit(solution)/shard_map/while/body/eval_jaxpr/reshape | solution.py:89
  144.8 2.3 fusion.52
  148.1 4.5 fusion.53
  152.8 8.7 %fusion.54 = (f32[4,8,128]{2,1,0:T(8,128)S(1)}, f32[4,8,128,512]{3,2,1,0:T(8,128)S(1)}) fusion(f32[4,8,128,512]{3,2,1,0:T(8,128)} %fusion.53, pred[4,512]{1,0:T(4,128)(4,1)S(1)} %broadcast_in_dim.57), kind=kOutput, calls=%fused_computation.65.clone.1 | output fusion | flops 12583423 | bytes 16795648 | tf_op jit(solution)/shard_map/while/body/eval_jaxpr/sub | solution.py:105
  164.5 5.4 gather_fusion
  169.9 7.4 %copy.61 = bf16[32,64,512]{1,0,2:T(8,128)(2,1)} copy(bf16[32,64,512]{2,1,0:T(8,128)(2,1)} %gather_fusion) | data formatting | bytes 4194304 | tf_op jit(solution)/shard_map/while/body/eval_jaxpr/gather | solution.py:89
  177.3 6.7 %reshape.153 = bf16[4,512,2,8,32]{1,0,4,3,2:T(4,128)(2,1)} reshape(bf16[32,64,512]{1,0,2:T(8,128)(2,1)} %copy.61) | data formatting | bytes 4194304 | tf_op jit(solution)/shard_map/while/body/eval_jaxpr/reshape | solution.py:89
  184.1 2.3 fusion.52
  187.4 4.5 fusion.53
  192.1 8.7 %fusion.54 = (f32[4,8,128]{2,1,0:T(8,128)S(1)}, f32[4,8,128,512]{3,2,1,0:T(8,128)S(1)}) fusion(f32[4,8,128,512]{3,2,1,0:T(8,128)} %fusion.53, pred[4,512]{1,0:T(4,128)(4,1)S(1)} %broadcast_in_dim.57), kind=kOutput, calls=%fused_computation.65.clone.1 | output fusion | flops 12583423 | bytes 16795648 | tf_op jit(solution)/shard_map/while/body/eval_jaxpr/sub | solution.py:105
  203.8 5.4 gather_fusion
  209.2 7.4 %copy.61 = bf16[32,64,512]{1,0,2:T(8,128)(2,1)} copy(bf16[32,64,512]{2,1,0:T(8,128)(2,1)} %gather_fusion) | data formatting | bytes 4194304 | tf_op jit(solution)/shard_map/while/body/eval_jaxpr/gather | solution.py:89
  216.6 6.7 %reshape.153 = bf16[4,512,2,8,32]{1,0,4,3,2:T(4,128)(2,1)} reshape(bf16[32,64,512]{1,0,2:T(8,128)(2,1)} %copy.61) | data formatting | bytes 4194304 | tf_op jit(solution)/shard_map/while/body/eval_jaxpr/reshape | solution.py:89
  223.4 2.3 fusion.52
  226.7 4.5 fusion.53
  231.4 8.7 %fusion.54 = (f32[4,8,128]{2,1,0:T(8,128)S(1)}, f32[4,8,128,512]{3,2,1,0:T(8,128)S(1)}) fusion(f32[4,8,128,512]{3,2,1,0:T(8,128)} %fusion.53, pred[4,512]{1,0:T(4,128)(4,1)S(1)} %broadcast_in_dim.57), kind=kOutput, calls=%fused_computation.65.clone.1 | output fusion | flops 12583423 | bytes 16795648 | tf_op jit(solution)/shard_map/while/body/eval_jaxpr/sub | solution.py:105
  243.1 5.4 gather_fusion
  248.5 7.4 %copy.61 = bf16[32,64,512]{1,0,2:T(8,128)(2,1)} copy(bf16[32,64,512]{2,1,0:T(8,128)(2,1)} %gather_fusion) | data formatting | bytes 4194304 | tf_op jit(solution)/shard_map/while/body/eval_jaxpr/gather | solution.py:89
  255.9 6.7 %reshape.153 = bf16[4,512,2,8,32]{1,0,4,3,2:T(4,128)(2,1)} reshape(bf16[32,64,512]{1,0,2:T(8,128)(2,1)} %copy.61) | data formatting | bytes 4194304 | tf_op jit(solution)/shard_map/while/body/eval_jaxpr/reshape | solution.py:89
  262.7 2.3 fusion.52
  266.0 4.5 fusion.53
  270.7 8.7 %fusion.54 = (f32[4,8,128]{2,1,0:T(8,128)S(1)}, f32[4,8,128,512]{3,2,1,0:T(8,128)S(1)}) fusion(f32[4,8,128,512]{3,2,1,0:T(8,128)} %fusion.53, pred[4,512]{1,0:T(4,128)(4,1)S(1)} %broadcast_in_dim.57), kind=kOutput, calls=%fused_computation.65.clone.1 | output fusion | flops 12583423 | bytes 16795648 | tf_op jit(solution)/shard_map/while/body/eval_jaxpr/sub | solution.py:105
  282.4 5.4 gather_fusion
  287.8 7.4 %copy.61 = bf16[32,64,512]{1,0,2:T(8,128)(2,1)} copy(bf16[32,64,512]{2,1,0:T(8,128)(2,1)} %gather_fusion) | data formatting | bytes 4194304 | tf_op jit(solution)/shard_map/while/body/eval_jaxpr/gather | solution.py:89
  295.2 6.7 %reshape.153 = bf16[4,512,2,8,32]{1,0,4,3,2:T(4,128)(2,1)} reshape(bf16[32,64,512]{1,0,2:T(8,128)(2,1)} %copy.61) | data formatting | bytes 4194304 | tf_op jit(solution)/shard_map/while/body/eval_jaxpr/reshape | solution.py:89
  302.0 2.3 fusion.52
  305.3 4.5 fusion.53
  310.0 8.7 %fusion.54 = (f32[4,8,128]{2,1,0:T(8,128)S(1)}, f32[4,8,128,512]{3,2,1,0:T(8,128)S(1)}) fusion(f32[4,8,128,512]{3,2,1,0:T(8,128)} %fusion.53, pred[4,512]{1,0:T(4,128)(4,1)S(1)} %broadcast_in_dim.57), kind=kOutput, calls=%fused_computation.65.clone.1 | output fusion | flops 12583423 | bytes 16795648 | tf_op jit(solution)/shard_map/while/body/eval_jaxpr/sub | solution.py:105
  321.7 5.4 gather_fusion
  327.1 7.4 %copy.61 = bf16[32,64,512]{1,0,2:T(8,128)(2,1)} copy(bf16[32,64,512]{2,1,0:T(8,128)(2,1)} %gather_fusion) | data formatting | bytes 4194304 | tf_op jit(solution)/shard_map/while/body/eval_jaxpr/gather | solution.py:89
  334.5 6.7 %reshape.153 = bf16[4,512,2,8,32]{1,0,4,3,2:T(4,128)(2,1)} reshape(bf16[32,64,512]{1,0,2:T(8,128)(2,1)} %copy.61) | data formatting | bytes 4194304 | tf_op jit(solution)/shard_map/while/body/eval_jaxpr/reshape | solution.py:89
  341.2 2.3 fusion.52
  344.6 4.5 fusion.53
  349.3 8.7 %fusion.54 = (f32[4,8,128]{2,1,0:T(8,128)S(1)}, f32[4,8,128,512]{3,2,1,0:T(8,128)S(1)}) fusion(f32[4,8,128,512]{3,2,1,0:T(8,128)} %fusion.53, pred[4,512]{1,0:T(4,128)(4,1)S(1)} %broadcast_in_dim.57), kind=kOutput, calls=%fused_computation.65.clone.1 | output fusion | flops 12583423 | bytes 16795648 | tf_op jit(solution)/shard_map/while/body/eval_jaxpr/sub | solution.py:105
  360.9 2.9 reshape.123
  363.8 3.0 multiply_reduce_fusion
  366.9 4.3 multiply_convert_fusion
  374.7 9.6 %fusion.19 = f32[256,512]{1,0:T(8,128)} fusion(f32[3072,512]{1,0:T(8,128)} %get-tuple-element.69, bf16[3072,256]{1,0:T(8,128)(2,1)S(1)} %bitcast.65, bf16[512,256]{1,0:T(8,128)(2,1)S(1)} %copy-done.4, f32[3072,256]{1,0:T(8,128)} %copy-done.2, f32[256]{0:T(256)S(1)} %bitcast.77, f32[3072]{0:T(1024)S(1)} %add_rsqrt_fusion), kind=kOutput, calls=%fused_computation.45 | convolution fusion | flops 1644429312 | bytes 11809792 | tf_op jit(solution)/shard_map/dot_general | solution.py:131
  384.3 5.0 fusion.18
  389.3 252.5 %all-reduce.3.cloned.1.call-done = (f32[256,512]{1,0:T(8,128)}, f32[512,256]{1,0:T(8,128)}) async-done(((f32[256,512]{1,0:T(8,128)}, f32[512,256]{1,0:T(8,128)}), (f32[256,512]{1,0:T(8,128)}, f32[512,256]{1,0:T(8,128)})) %all-reduce.3.cloned.1.call-update) | async-done | bytes 1048592 | tf_op jit(solution)/shard_map/psum | solution.py:132
  (97 shorter events, 43.3 us)
Async XLA Ops:
  7.2 364.0 %copy-start = (bf16[1,24,128,256]{3,2,1,0:T(8,128)(2,1)S(1)}, bf16[1,24,128,256]{3,2,1,0:T(8,128)(2,1)}, u32[]{:S(2)}) copy-start(bf16[1,24,128,256]{3,2,1,0:T(8,128)(2,1)} %param.27) | copy-start | bytes 4718596
  7.2 105.5 %all-gather.3.cloned.1.call-start = ((), (), s32[]{:S(2)}) async-start(), calls=%async_computation | async-start | bytes 17039360 | tf_op jit(solution)/shard_map/all_gather | solution.py:65
  9.3 632.6 %all-reduce.3.cloned.1.call-start = ((), (), s32[]{:S(2)}) async-start(), calls=%async_computation.1 | async-start | bytes 2097152 | tf_op jit(solution)/shard_map/psum | solution.py:132
  9.3 63.4 %collective-permute-start = (bf16[24,128,256]{2,1,0:T(8,128)(2,1)}, bf16[24,128,256]{2,1,0:T(8,128)(2,1)S(1)}, u32[]{:S(2)}, u32[]{:S(2)}) collective-permute-start(bf16[24,128,256]{2,1,0:T(8,128)(2,1)} %bitcast.70), channel_id=1, source_target_pairs={{0,1},{1,2},{2,3},{3,4},{4,5},{5,6},{6,7},{7,8},{8,9},{9,10},{10,1... | collective-permute-start | bytes 4718600 | tf_op jit(solution)/shard_map/ppermute | solution.py:12
  75.6 1.7 copy-start.1
  75.7 2.2 copy-start.6
  360.9 2.9 copy-start.5
  363.8 3.1 copy-start.7
  366.8 4.4 copy-start.2
  371.2 1.7 copy-start.3
  371.2 3.5 copy-start.4
Sparse Core Ops, SparseCore 0:
  11.3 101.2 all-gather.2
  384.5 257.3 all-reduce.2
where the time goes:
time: 655 us; the launch traced here: 652 us
  waiting for transfers between devices  281 us (43%)
  local copies, waits for them, and re-layouts  175 us (27%)
  matrix products  65.4 us (10%)
  blocking collectives  58.8 us (9%)
  other arithmetic  55.9 us (9%)
  between operations  14.8 us (2%)
    psum x1, waiting for transfers between devices, on_device(): lax.psum((part_w_in, part_w_out), ('drive', 'brick'))  253 us
    gather x12, local copies, waits for them, and re-layouts, attend(): keyval[jnp.maximum(entry_block, 0)]  76.8 us
    all_gather x1, blocking collectives, on_device(): lax.all_gather(tile_sends[0], 'brick', axis=1, tiled=True)  58.8 us
    sub x6, other arithmetic, attend(): raised = jnp.exp(scores - row_peak)  52.4 us
    reshape x6, local copies, waits for them, and re-layouts, attend(): keyval[jnp.maximum(entry_block, 0)]  40.4 us
    all_gather x1, waiting for transfers between devices, on_device(): lax.all_gather(payload, 'brick', axis=1, tiled=True)  28 us
    dot_general x6, matrix products, attend(): jnp.einsum('gqhd,gkhd->ghqk', query_block, keys_part, preferred_element_t...  27.2 us
    slice x6, local copies, waits for them, and re-layouts, attend(): values_part = gathered[:, :, 1]  13.6 us
  transfers between devices with their start and end apart: 3, of which 2 were waited for; matrix products, arithmetic and copies ran while one was open for 3% of the time, Pallas kernels for 0%

commit v1 on v0

--- a/solution.py
+++ b/solution.py
@@ -4,6 +4,9 @@
 from jax.sharding import PartitionSpec as P
 
 HD = 32
+group_the_sector = lambda inp, ndim_at: jnp.concatenate(
+    lax.all_to_all(jnp.stack(lax.axis_size("brick") * [inp], 0), "brick", 0, 0), ndim_at
+)
 
 
 def passed_along(value, axis, by):
@@ -62,7 +65,7 @@
         .reshape(frames, tile_dev, pixels, 2 * width)
     )
     everything, all_plans = (
-        lax.all_gather(payload, "brick", axis=1, tiled=True),
+        group_the_sector(payload, 1),
         lax.all_gather(tile_sends[0], "brick", axis=1, tiled=True),
     )
     own_plan = lax.dynamic_slice_in_dim(all_plans, own_index * capacity, capacity, 2)

time: 655 us -> 989 us (1.51)
  blocking collectives: 58.8 us -> 404 us
  waiting for transfers between devices: 281 us -> 253 us
  starting transfers between devices: 2 us -> 14.4 us
    all_gather x1, blocking collectives: 58.8 us -> 404 us  [on_device(): lax.all_gather(tile_sends[0], 'brick', axis=1, tiled=True)]
    all_gather x1 -> x0, waiting for transfers between devices: 28 us -> none  [on_device(): lax.all_gather(payload, 'brick', axis=1, tiled=True)]
    all_to_all x0 -> x1, starting transfers between devices: none -> 12.4 us  [lax.all_to_all(jnp.stack(lax.axis_size('brick') * [inp], 0), 'brick', 0, 0)]
  transfers between devices with their start and end apart: 3 -> 3, of which waited for: 2 -> 1; matrix products, arithmetic and copies ran while one was open for 3% -> 2% of each run, Pallas kernels for 0% -> 0%
where the time goes in v1:
time: 989 us; the launch traced here: 987 us
  blocking collectives  404 us (41%)
  waiting for transfers between devices  253 us (26%)
  local copies, waits for them, and re-layouts  180 us (18%)
  matrix products  64.6 us (7%)
  other arithmetic  55.7 us (6%)
  between operations  14.9 us (2%)
  starting transfers between devices  14.4 us (1%)
    all_gather x1, blocking collectives, on_device(): lax.all_gather(tile_sends[0], 'brick', axis=1, tiled=True)  404 us
    psum x1, waiting for transfers between devices, on_device(): lax.psum((part_w_in, part_w_out), ('drive', 'brick'))  253 us
    gather x12, local copies, waits for them, and re-layouts, attend(): keyval[jnp.maximum(entry_block, 0)]  77.1 us
    sub x6, other arithmetic, attend(): raised = jnp.exp(scores - row_peak)  52.4 us
    reshape x6, local copies, waits for them, and re-layouts, attend(): keyval[jnp.maximum(entry_block, 0)]  40.4 us
    dot_general x6, matrix products, attend(): jnp.einsum('gqhd,gkhd->ghqk', query_block, keys_part, preferred_element_t...  27.1 us
  transfers between devices with their start and end apart: 3, of which 1 were waited for; matrix products, arithmetic and copies ran while one was open for 2% of the time, Pallas kernels for 0%

profile of v1, /device:TPU:2, one launch (start us, length us, event | category | flops | bytes accessed | tf_op | source)
XLA Modules:
  0.0 986.7 jit_solution(7081520909274607711)
XLA Ops:
  8.5 6.0 stack.3
  14.6 12.4 %all-to-all-start = ((bf16[64,1,4,64,512]{4,3,2,1,0:T(8,128)(2,1)}), bf16[64,1,4,64,512]{4,3,2,1,0:T(8,128)(2,1)}, u32[]{:S(2)}, u32[]{:S(2)}) async-start(bf16[64,1,4,64,512]{4,3,2,1,0:T(8,128)(2,1)} %stack.3), calls=%async_computation | async-start | bytes 33554432 | tf_op jit(solution)/shard_map/all_to_all | solution.py:8
  29.7 404.4 %all-gather = s32[1,64,1,128]{3,2,0,1:T(1,128)S(1)} all-gather(s32[1,1,1,128]{3,2,0,1:T(1,128)S(1)} %bitcast.77), channel_id=2, replica_groups=mesh['drive'=4,'brick'=64] {'brick'}, dimensions={1}, use_global_device_ids=true | all-gather | bytes 33280 | tf_op jit(solution)/shard_map/all_gather | solution.py:69
  434.8 2.6 multiply_reduce_fusion.1
  442.0 4.2 reshape.126
  446.2 12.5 %gather_fusion.1 = bf16[128,64,512]{2,1,0:T(8,128)(2,1)} fusion(bf16[1,256,64,512]{3,2,1,0:T(8,128)(2,1)} %bitcast.13, s32[128]{0:T(128)S(1)} %or_bitcast_fusion), kind=kCustom, calls=%fused_computation.1 | custom fusion | bytes 16778240 | tf_op jit(solution)/shard_map/vmap()/gather | solution.py:28
  458.7 236.0 %while.10 = (s32[]{:T(128)}, bf16[6,4,128,8,32]{2,1,0,4,3:T(4,128)(2,1)}, s32[6,4,8]{2,1,0:T(4,128)S(1)}, bf16[128,64,512]{2,1,0:T(8,128)(2,1)}, bf16[6,4,128,8,32]{2,1,0,4,3:T(4,128)(2,1)}, /*index=5*/s32[]{:T(128)}) while((s32[]{:T(128)}, bf16[6,4,128,8,32]{2,1,0,4,3:T(4,128)(2,1)}, s32[6,4,8]{2,1,0:T(4,128)S(1)}, ...), condition=%wide.region_4.5_spmd, body=%wide.region_1.4_spmd.sunk | while | flops 285345344 | bytes 54048272 | solution.py:115
  458.8 5.4 gather_fusion
  464.2 7.4 copy.60
  471.6 6.7 reshape.157
  478.4 2.3 fusion.52
  481.7 4.5 fusion.53
  486.4 8.7 fusion.54
  498.1 5.4 gather_fusion
  503.5 7.4 copy.60
  511.0 6.7 reshape.157
  517.7 2.3 fusion.52
  521.0 4.5 fusion.53
  525.7 8.7 fusion.54
  537.4 5.4 gather_fusion
  542.9 7.4 copy.60
  550.3 6.7 reshape.157
  557.0 2.3 fusion.52
  560.4 4.5 fusion.53
  565.0 8.7 fusion.54
  576.8 5.4 gather_fusion
  582.2 7.4 copy.60
  589.6 6.7 reshape.157
  596.4 2.3 fusion.52
  599.7 4.5 fusion.53
  604.4 8.7 fusion.54
  616.1 5.4 gather_fusion
  621.5 7.4 copy.60
  629.0 6.7 reshape.157
  639.0 4.5 fusion.53
  643.7 8.7 fusion.54
  655.5 5.4 gather_fusion
  660.9 7.4 copy.60
  668.3 6.7 reshape.157
  675.0 2.3 fusion.52
  678.4 4.5 fusion.53
  683.0 8.7 fusion.54
  694.7 2.9 reshape.127
  697.6 3.0 multiply_reduce_fusion
  700.7 4.3 multiply_convert_fusion
  708.4 9.6 fusion.19
  718.1 5.0 fusion.18
  723.1 253.0 %all-reduce.3.cloned.1.call-done = (f32[256,512]{1,0:T(8,128)}, f32[512,256]{1,0:T(8,128)}) async-done(((f32[256,512]{1,0:T(8,128)}, f32[512,256]{1,0:T(8,128)}), (f32[256,512]{1,0:T(8,128)}, f32[512,256]{1,0:T(8,128)})) %all-reduce.3.cloned.1.call-update) | async-done | bytes 1048592 | tf_op jit(solution)/shard_map/psum | solution.py:135
  (105 shorter events, 43.4 us)
Async XLA Ops:
  7.2 697.8 %copy-start = (bf16[1,24,128,256]{3,2,1,0:T(8,128)(2,1)S(1)}, bf16[1,24,128,256]{3,2,1,0:T(8,128)(2,1)}, u32[]{:S(2)}) copy-start(bf16[1,24,128,256]{3,2,1,0:T(8,128)(2,1)} %param.27) | copy-start | bytes 4718596
  14.6 12.4 %copy-start.4 = (bf16[1,24,128,256]{3,2,1,0:T(8,128)(2,1)S(1)}, bf16[1,24,128,256]{3,2,1,0:T(8,128)(2,1)}, u32[]{:S(2)}) copy-start(bf16[1,24,128,256]{3,2,1,0:T(8,128)(2,1)} %param.17) | copy-start | bytes 4718596
  14.6 15.1 %copy-start.10 = (s32[1,1,1,128]{3,2,1,0:T(1,128)S(1)}, s32[1,1,1,128]{3,2,1,0:T(1,128)}, u32[]{:S(2)}) copy-start(s32[1,1,1,128]{3,2,1,0:T(1,128)} %param.18) | copy-start | bytes 1540
  14.6 420.0 %copy-start.8 = (s32[1,1,24,8]{2,3,1,0:T(8,128)S(1)}, s32[1,1,24,8]{2,3,1,0:T(8,128)}, u32[]{:S(2)}) copy-start(s32[1,1,24,8]{2,3,1,0:T(8,128)} %param.19) | copy-start | bytes 2308
  14.6 420.2 %copy-start.9 = (f32[2,256]{1,0:T(2,128)S(1)}, f32[2,256]{1,0:T(2,128)}, u32[]{:S(2)}) copy-start(f32[2,256]{1,0:T(2,128)} %param.21) | copy-start | bytes 6148
  14.6 431.6 %all-to-all-start = ((bf16[64,1,4,64,512]{4,3,2,1,0:T(8,128)(2,1)}), bf16[64,1,4,64,512]{4,3,2,1,0:T(8,128)(2,1)}, u32[]{:S(2)}, u32[]{:S(2)}) async-start(bf16[64,1,4,64,512]{4,3,2,1,0:T(8,128)(2,1)} %stack.3), calls=%async_computation | async-start | bytes 33554432 | tf_op jit(solution)/shard_map/all_to_all | solution.py:8
  26.9 949.2 %all-reduce.3.cloned.1.call-start = ((), (), s32[]{:S(2)}) async-start(), calls=%async_computation.1 | async-start | bytes 2097152 | tf_op jit(solution)/shard_map/psum | solution.py:135
  27.0 407.8 %collective-permute-start = (bf16[24,128,256]{2,1,0:T(8,128)(2,1)S(1)}, bf16[24,128,256]{2,1,0:T(8,128)(2,1)}, u32[]{:S(2)}, u32[]{:S(2)}) collective-permute-start(bf16[24,128,256]{2,1,0:T(8,128)(2,1)S(1)} %bitcast.69), channel_id=1, source_target_pairs={{0,1},{1,2},{2,3},{3,4},{4,5},{5,6},{6,7},{7,8},{8,9},{9,10},{10,1... | collective-permute-start | bytes 4718600 | tf_op jit(solution)/shard_map/ppermute | solution.py:15
  437.4 1.6 copy-start.1
  437.4 2.1 copy-start.7
  694.7 2.9 copy-start.6
  697.6 3.1 copy-start.11
  700.6 4.3 copy-start.2
  705.0 1.6 copy-start.3
  705.0 3.5 copy-start.5
Sparse Core Ops, SparseCore 0:
  718.2 257.8 all-reduce.2
